TPU v7x, 128 devices: a whole 4x4x4 slice. The times are simulated.
128 devices in a mesh: stream: 4 (over x), cross: 32 (over z, y, core).
Axes of the slice: x: 4, y: 4, z: 4, core: 2. Of those that a mesh axis runs over, the one named last changes fastest.
Arguments:
- forcing: float32 [16, 32, 4096], P('stream', None, 'cross'), may hold values from -6 to 6
- cotangent: float32 [16, 32, 4096], P('stream', None, 'cross'), may hold values from -6 to 6
- inverses: float32 [16, 4096, 4096], P('stream', 'cross'), as said below
- flags: int32 [16, 2048], P('stream', 'cross'), may hold values from 0 to 2
Outputs:
- response: float32 [16, 32, 4096], P('stream', None, 'cross')
- forcing_grad: float32 [16, 32, 4096], P('stream', None, 'cross')
Inputs may be any that keep to these rules, and one draw needn't show every extreme that they name: `inverses`: each layer's inverse is the real form of a complex 2048 x 2048 matrix: entries (2i, 2j) and (2i+1, 2j+1) are equal, entry (2i, 2j+1) is the negative of entry (2i+1, 2j).
All inputs are finite; a program needn't handle non-finite values.
Results may differ from a plain program's by a relative error of at most 0.00015.
Values sent between devices are 32-bit elements; how exact they have to be, the bound alone decides.
A program may use at most 64 MiB of HBM per device.

v0:
```python
import jax
import jax.numpy as jnp
from jax import lax
from jax.sharding import PartitionSpec as P


def joined_along(blocks, dim):
    blocks = jnp.moveaxis(blocks, 0, dim)
    dims = blocks.shape
    return blocks.reshape(*dims[:dim], dims[dim] * dims[dim + 1], *dims[dim + 2 :])


def copy_for_each(value, axis):
    copies = jnp.broadcast_to(value, (lax.axis_size(axis), *value.shape))
    return lax.all_to_all(copies, axis, split_axis=0, concat_axis=0, tiled=True)


def gather_directly(value, axis, dim):
    return joined_along(copy_for_each(value, axis), dim)


def split_up(value, dim, size):
    dims = value.shape
    blocks = value.reshape(*dims[:dim], size, dims[dim] // size, *dims[dim + 1 :])
    return jnp.moveaxis(blocks, dim, 0)


def summed_on_arrival(value, axis, dim):
    blocks = split_up(value, dim, lax.axis_size(axis))
    arrived = lax.all_to_all(blocks, axis, split_axis=0, concat_axis=0, tiled=True)
    return arrived.sum(axis=0)


def shifted(block, axis, distance):
    devices = range(lax.axis_size(axis))
    route = [(i - distance, i) for i in devices if i - distance in devices]
    return lax.ppermute(block, axis, route)


def penalty(flag_cells):
    factor = jnp.where(flag_cells == 0, 0.98, jnp.where(flag_cells == 1, 0.05, 0.5)).astype(
        jnp.float32
    )
    return jnp.repeat(factor, 2, axis=-1)


def forward_apply(matrix, source):
    return lax.dot_general(
        gather_directly(source, "cross", 1),
        matrix,
        (((1,), (1,)), ((), ())),
        precision=lax.Precision.HIGHEST,
        preferred_element_type=jnp.float32,
    )


def backward_apply(matrix, source):
    share = summed_on_arrival(
        lax.dot_general(
            matrix,
            source,
            (((0,), (1,)), ((), ())),
            precision=lax.Precision.HIGHEST,
            preferred_element_type=jnp.float32,
        ),
        "cross",
        0,
    )
    return jnp.transpose(share)


def shards(forcing, cotangent, inverses, flags):
    local_layers = inverses.shape[0]
    row_count = inverses.shape[1]
    vectors = forcing.shape[1]
    sections = lax.axis_size("stream")
    factors = penalty(flags)
    groups = 1
    total_turns = sections + groups - 1
    blank = jnp.zeros((vectors, row_count), jnp.float32)
    blank_all = jnp.zeros((local_layers, vectors, row_count), jnp.float32)

    def forward_turn(state):
        incoming, response = state
        carried = incoming
        for layer in range(local_layers):
            drive = forcing[layer]
            source = drive + factors[layer] * carried
            carried = forward_apply(inverses[layer], source)
            response = response.at[layer].set(carried)
        passed = shifted(carried, "stream", 1)
        incoming = passed
        return (incoming, response)

    def backward_turn(state):
        incoming, gradient_all = state
        carried = incoming
        for layer in range(local_layers - 1, -1, -1):
            sink = cotangent[layer]
            gradient = backward_apply(inverses[layer], sink + carried)
            gradient_all = gradient_all.at[layer].set(gradient)
            carried = factors[layer] * gradient
        passed = shifted(carried, "stream", -1)
        incoming = passed
        return (incoming, gradient_all)

    def joint_turn(moment, state):
        return (forward_turn(state[0]), backward_turn(state[1]))

    forward_state, backward_state = lax.fori_loop(
        0, total_turns, joint_turn, ((blank, blank_all), (blank, blank_all))
    )
    return (forward_state[1], backward_state[1])


def solution(mesh):
    in_specs = (
        P("stream", None, "cross"),
        P("stream", None, "cross"),
        P("stream", "cross", None),
        P("stream", "cross"),
    )
    out_specs = (P("stream", None, "cross"), P("stream", None, "cross"))
    return jax.shard_map(shards, mesh=mesh, in_specs=in_specs, out_specs=out_specs, check_vma=False)
```

profile of v0, /device:TPU:1, one launch (start us, length us, event | category | flops | bytes accessed | tf_op | source)
XLA Modules:
  0.0 637.3 jit_solution(11819742718779583434)
XLA Ops:
  1.6 635.1 %while.27 = (s32[]{:T(128)}, f32[32,128]{1,0:T(8,128)S(1)}, f32[4,32,128]{2,1,0:T(8,128)S(1)}, f32[32,128]{1,0:T(8,128)S(1)}, f32[4,32,128]{2,1,0:T(8,128)S(1)},...) while((s32[]{:T(128)}, f32[32,128]{1,0:T(8,128)S(1)}, ...), condition=%wide.region_5.6_spmd, body=%wide.region_0.5_spmd.sunk | while | flops 1611186176 | bytes 41262980 | solution.py:110
  29.2 15.1 %all_to_all.80 = f32[32,128,32]{1,2,0:T(8,128)S(1)} all-to-all(f32[32,128,32]{1,2,0:T(8,128)S(1)} %bitcast.260), channel_id=1, replica_groups=mesh['stream'=4,'cross'=32] {'cross'}, dimensions={0} | all-to-all | bytes 1048576 | tf_op jit(solution)/shard_map/while/body/eval_jaxpr/all_to_all | solution.py:30
  47.1 15.1 %all_to_all.81 = f32[32,128,32]{1,2,0:T(8,128)S(1)} all-to-all(f32[32,128,32]{1,2,0:T(8,128)S(1)} %bitcast.261), channel_id=1, replica_groups=mesh['stream'=4,'cross'=32] {'cross'}, dimensions={0} | all-to-all | bytes 1048576 | tf_op jit(solution)/shard_map/while/body/eval_jaxpr/all_to_all | solution.py:30
  65.1 15.1 %all_to_all.82 = f32[32,128,32]{1,2,0:T(8,128)S(1)} all-to-all(f32[32,128,32]{1,2,0:T(8,128)S(1)} %bitcast.262), channel_id=1, replica_groups=mesh['stream'=4,'cross'=32] {'cross'}, dimensions={0} | all-to-all | bytes 1048576 | tf_op jit(solution)/shard_map/while/body/eval_jaxpr/all_to_all | solution.py:30
  80.3 15.1 %all_to_all.83 = f32[32,32,128]{2,1,0:T(8,128)S(1)} all-to-all(f32[32,32,128]{2,1,0:T(8,128)S(1)} %broadcast_in_dim.62), channel_id=1, replica_groups=mesh['stream'=4,'cross'=32] {'cross'}, dimensions={0} | all-to-all | bytes 1048576 | tf_op jit(solution)/shard_map/while/body/eval_jaxpr/all_to_all | solution.py:15
  103.9 11.5 %all-to-all-done.5 = f32[32,32,128]{2,1,0:T(8,128)S(1)} async-done(((f32[32,32,128]{2,1,0:T(8,128)}), f32[32,32,128]{2,1,0:T(8,128)S(1)}, u32[]{:S(2)}, u32[]{:S(2)}) %all-to-all-start.5) | async-done | bytes 524320 | tf_op jit(solution)/shard_map/while/body/eval_jaxpr/all_to_all | solution.py:15
  171.8 11.5 %all-to-all-done = f32[32,128,32]{1,2,0:T(8,128)S(1)} async-done(((f32[32,128,32]{1,2,0:T(8,128)}), f32[32,128,32]{1,2,0:T(8,128)S(1)}, u32[]{:S(2)}, u32[]{:S(2)}) %all-to-all-start) | async-done | bytes 524320 | tf_op jit(solution)/shard_map/while/body/eval_jaxpr/all_to_all | solution.py:30
  186.2 15.1 %all_to_all.80 = f32[32,128,32]{1,2,0:T(8,128)S(1)} all-to-all(f32[32,128,32]{1,2,0:T(8,128)S(1)} %bitcast.260), channel_id=1, replica_groups=mesh['stream'=4,'cross'=32] {'cross'}, dimensions={0} | all-to-all | bytes 1048576 | tf_op jit(solution)/shard_map/while/body/eval_jaxpr/all_to_all | solution.py:30
  204.1 15.1 %all_to_all.81 = f32[32,128,32]{1,2,0:T(8,128)S(1)} all-to-all(f32[32,128,32]{1,2,0:T(8,128)S(1)} %bitcast.261), channel_id=1, replica_groups=mesh['stream'=4,'cross'=32] {'cross'}, dimensions={0} | all-to-all | bytes 1048576 | tf_op jit(solution)/shard_map/while/body/eval_jaxpr/all_to_all | solution.py:30
  222.1 15.1 %all_to_all.82 = f32[32,128,32]{1,2,0:T(8,128)S(1)} all-to-all(f32[32,128,32]{1,2,0:T(8,128)S(1)} %bitcast.262), channel_id=1, replica_groups=mesh['stream'=4,'cross'=32] {'cross'}, dimensions={0} | all-to-all | bytes 1048576 | tf_op jit(solution)/shard_map/while/body/eval_jaxpr/all_to_all | solution.py:30
  237.3 15.1 %all_to_all.83 = f32[32,32,128]{2,1,0:T(8,128)S(1)} all-to-all(f32[32,32,128]{2,1,0:T(8,128)S(1)} %broadcast_in_dim.62), channel_id=1, replica_groups=mesh['stream'=4,'cross'=32] {'cross'}, dimensions={0} | all-to-all | bytes 1048576 | tf_op jit(solution)/shard_map/while/body/eval_jaxpr/all_to_all | solution.py:15
  260.9 11.5 %all-to-all-done.5 = f32[32,32,128]{2,1,0:T(8,128)S(1)} async-done(((f32[32,32,128]{2,1,0:T(8,128)}), f32[32,32,128]{2,1,0:T(8,128)S(1)}, u32[]{:S(2)}, u32[]{:S(2)}) %all-to-all-start.5) | async-done | bytes 524320 | tf_op jit(solution)/shard_map/while/body/eval_jaxpr/all_to_all | solution.py:15
  329.6 11.5 %all-to-all-done = f32[32,128,32]{1,2,0:T(8,128)S(1)} async-done(((f32[32,128,32]{1,2,0:T(8,128)}), f32[32,128,32]{1,2,0:T(8,128)S(1)}, u32[]{:S(2)}, u32[]{:S(2)}) %all-to-all-start) | async-done | bytes 524320 | tf_op jit(solution)/shard_map/while/body/eval_jaxpr/all_to_all | solution.py:30
  344.0 15.1 %all_to_all.80 = f32[32,128,32]{1,2,0:T(8,128)S(1)} all-to-all(f32[32,128,32]{1,2,0:T(8,128)S(1)} %bitcast.260), channel_id=1, replica_groups=mesh['stream'=4,'cross'=32] {'cross'}, dimensions={0} | all-to-all | bytes 1048576 | tf_op jit(solution)/shard_map/while/body/eval_jaxpr/all_to_all | solution.py:30
  361.9 15.1 %all_to_all.81 = f32[32,128,32]{1,2,0:T(8,128)S(1)} all-to-all(f32[32,128,32]{1,2,0:T(8,128)S(1)} %bitcast.261), channel_id=1, replica_groups=mesh['stream'=4,'cross'=32] {'cross'}, dimensions={0} | all-to-all | bytes 1048576 | tf_op jit(solution)/shard_map/while/body/eval_jaxpr/all_to_all | solution.py:30
  379.9 15.1 %all_to_all.82 = f32[32,128,32]{1,2,0:T(8,128)S(1)} all-to-all(f32[32,128,32]{1,2,0:T(8,128)S(1)} %bitcast.262), channel_id=1, replica_groups=mesh['stream'=4,'cross'=32] {'cross'}, dimensions={0} | all-to-all | bytes 1048576 | tf_op jit(solution)/shard_map/while/body/eval_jaxpr/all_to_all | solution.py:30
  395.1 15.1 %all_to_all.83 = f32[32,32,128]{2,1,0:T(8,128)S(1)} all-to-all(f32[32,32,128]{2,1,0:T(8,128)S(1)} %broadcast_in_dim.62), channel_id=1, replica_groups=mesh['stream'=4,'cross'=32] {'cross'}, dimensions={0} | all-to-all | bytes 1048576 | tf_op jit(solution)/shard_map/while/body/eval_jaxpr/all_to_all | solution.py:15
  418.7 11.5 %all-to-all-done.5 = f32[32,32,128]{2,1,0:T(8,128)S(1)} async-done(((f32[32,32,128]{2,1,0:T(8,128)}), f32[32,32,128]{2,1,0:T(8,128)S(1)}, u32[]{:S(2)}, u32[]{:S(2)}) %all-to-all-start.5) | async-done | bytes 524320 | tf_op jit(solution)/shard_map/while/body/eval_jaxpr/all_to_all | solution.py:15
  487.4 11.5 %all-to-all-done = f32[32,128,32]{1,2,0:T(8,128)S(1)} async-done(((f32[32,128,32]{1,2,0:T(8,128)}), f32[32,128,32]{1,2,0:T(8,128)S(1)}, u32[]{:S(2)}, u32[]{:S(2)}) %all-to-all-start) | async-done | bytes 524320 | tf_op jit(solution)/shard_map/while/body/eval_jaxpr/all_to_all | solution.py:30
  501.8 15.1 %all_to_all.80 = f32[32,128,32]{1,2,0:T(8,128)S(1)} all-to-all(f32[32,128,32]{1,2,0:T(8,128)S(1)} %bitcast.260), channel_id=1, replica_groups=mesh['stream'=4,'cross'=32] {'cross'}, dimensions={0} | all-to-all | bytes 1048576 | tf_op jit(solution)/shard_map/while/body/eval_jaxpr/all_to_all | solution.py:30
  519.8 15.1 %all_to_all.81 = f32[32,128,32]{1,2,0:T(8,128)S(1)} all-to-all(f32[32,128,32]{1,2,0:T(8,128)S(1)} %bitcast.261), channel_id=1, replica_groups=mesh['stream'=4,'cross'=32] {'cross'}, dimensions={0} | all-to-all | bytes 1048576 | tf_op jit(solution)/shard_map/while/body/eval_jaxpr/all_to_all | solution.py:30
  537.7 15.1 %all_to_all.82 = f32[32,128,32]{1,2,0:T(8,128)S(1)} all-to-all(f32[32,128,32]{1,2,0:T(8,128)S(1)} %bitcast.262), channel_id=1, replica_groups=mesh['stream'=4,'cross'=32] {'cross'}, dimensions={0} | all-to-all | bytes 1048576 | tf_op jit(solution)/shard_map/while/body/eval_jaxpr/all_to_all | solution.py:30
  552.9 15.1 %all_to_all.83 = f32[32,32,128]{2,1,0:T(8,128)S(1)} all-to-all(f32[32,32,128]{2,1,0:T(8,128)S(1)} %broadcast_in_dim.62), channel_id=1, replica_groups=mesh['stream'=4,'cross'=32] {'cross'}, dimensions={0} | all-to-all | bytes 1048576 | tf_op jit(solution)/shard_map/while/body/eval_jaxpr/all_to_all | solution.py:15
  576.5 11.5 %all-to-all-done.5 = f32[32,32,128]{2,1,0:T(8,128)S(1)} async-done(((f32[32,32,128]{2,1,0:T(8,128)}), f32[32,32,128]{2,1,0:T(8,128)S(1)}, u32[]{:S(2)}, u32[]{:S(2)}) %all-to-all-start.5) | async-done | bytes 524320 | tf_op jit(solution)/shard_map/while/body/eval_jaxpr/all_to_all | solution.py:15
  (185 shorter events, 313.9 us)
Async XLA Ops:
  5.3 21.0 %all-to-all-start = ((f32[32,128,32]{1,2,0:T(8,128)}), f32[32,128,32]{1,2,0:T(8,128)S(1)}, u32[]{:S(2)}, u32[]{:S(2)}) async-start(f32[32,128,32]{1,2,0:T(8,128)} %bitcast.256), calls=%async_computation | async-start | bytes 1048576 | tf_op jit(solution)/shard_map/while/body/eval_jaxpr/all_to_all | solution.py:30
  99.9 15.5 %all-to-all-start.5 = ((f32[32,32,128]{2,1,0:T(8,128)}), f32[32,32,128]{2,1,0:T(8,128)S(1)}, u32[]{:S(2)}, u32[]{:S(2)}) async-start(f32[32,32,128]{2,1,0:T(8,128)} %broadcast_in_dim.63), calls=%async_computation.5 | async-start | bytes 1048576 | tf_op jit(solution)/shard_map/while/body/eval_jaxpr/all_to_all | solution.py:15
  120.0 15.5 %all-to-all-start.6 = ((f32[32,32,128]{2,1,0:T(8,128)}), f32[32,32,128]{2,1,0:T(8,128)S(1)}, u32[]{:S(2)}, u32[]{:S(2)}) async-start(f32[32,32,128]{2,1,0:T(8,128)} %broadcast_in_dim.64), calls=%async_computation.6 | async-start | bytes 1048576 | tf_op jit(solution)/shard_map/while/body/eval_jaxpr/all_to_all | solution.py:15
  124.0 38.4 %collective-permute-start.1 = (f32[32,128]{1,0:T(8,128)S(1)}, f32[32,128]{1,0:T(8,128)S(1)}, u32[]{:S(2)}, u32[]{:S(2)}) collective-permute-start(f32[32,128]{1,0:T(8,128)S(1)} %get-tuple-element.383), channel_id=1, source_target_pairs={{32,0},{64,32},{96,64},{33,1},{65,33},{97,65},{34,2},{66,34},{98,6... | collective-permute-start | bytes 49160 | tf_op jit(solution)/shard_map/while/body/eval_jaxpr/ppermute | solution.py:37
  140.1 15.5 %all-to-all-start.7 = ((f32[32,32,128]{2,1,0:T(8,128)}), f32[32,32,128]{2,1,0:T(8,128)S(1)}, u32[]{:S(2)}, u32[]{:S(2)}) async-start(f32[32,32,128]{2,1,0:T(8,128)} %broadcast_in_dim.65), calls=%async_computation.7 | async-start | bytes 1048576 | tf_op jit(solution)/shard_map/while/body/eval_jaxpr/all_to_all | solution.py:15
  159.3 4.0 collective-permute-start
  166.9 16.3 %all-to-all-start = ((f32[32,128,32]{1,2,0:T(8,128)}), f32[32,128,32]{1,2,0:T(8,128)S(1)}, u32[]{:S(2)}, u32[]{:S(2)}) async-start(f32[32,128,32]{1,2,0:T(8,128)} %bitcast.256), calls=%async_computation | async-start | bytes 1048576 | tf_op jit(solution)/shard_map/while/body/eval_jaxpr/all_to_all | solution.py:30
  256.9 15.5 %all-to-all-start.5 = ((f32[32,32,128]{2,1,0:T(8,128)}), f32[32,32,128]{2,1,0:T(8,128)S(1)}, u32[]{:S(2)}, u32[]{:S(2)}) async-start(f32[32,32,128]{2,1,0:T(8,128)} %broadcast_in_dim.63), calls=%async_computation.5 | async-start | bytes 1048576 | tf_op jit(solution)/shard_map/while/body/eval_jaxpr/all_to_all | solution.py:15
  277.0 15.5 %all-to-all-start.6 = ((f32[32,32,128]{2,1,0:T(8,128)}), f32[32,32,128]{2,1,0:T(8,128)S(1)}, u32[]{:S(2)}, u32[]{:S(2)}) async-start(f32[32,32,128]{2,1,0:T(8,128)} %broadcast_in_dim.64), calls=%async_computation.6 | async-start | bytes 1048576 | tf_op jit(solution)/shard_map/while/body/eval_jaxpr/all_to_all | solution.py:15
  281.0 39.3 %collective-permute-start.1 = (f32[32,128]{1,0:T(8,128)S(1)}, f32[32,128]{1,0:T(8,128)S(1)}, u32[]{:S(2)}, u32[]{:S(2)}) collective-permute-start(f32[32,128]{1,0:T(8,128)S(1)} %get-tuple-element.383), channel_id=1, source_target_pairs={{32,0},{64,32},{96,64},{33,1},{65,33},{97,65},{34,2},{66,34},{98,6... | collective-permute-start | bytes 49160 | tf_op jit(solution)/shard_map/while/body/eval_jaxpr/ppermute | solution.py:37
  297.1 15.5 %all-to-all-start.7 = ((f32[32,32,128]{2,1,0:T(8,128)}), f32[32,32,128]{2,1,0:T(8,128)S(1)}, u32[]{:S(2)}, u32[]{:S(2)}) async-start(f32[32,32,128]{2,1,0:T(8,128)} %broadcast_in_dim.65), calls=%async_computation.7 | async-start | bytes 1048576 | tf_op jit(solution)/shard_map/while/body/eval_jaxpr/all_to_all | solution.py:15
  316.3 4.8 collective-permute-start
  324.8 16.3 %all-to-all-start = ((f32[32,128,32]{1,2,0:T(8,128)}), f32[32,128,32]{1,2,0:T(8,128)S(1)}, u32[]{:S(2)}, u32[]{:S(2)}) async-start(f32[32,128,32]{1,2,0:T(8,128)} %bitcast.256), calls=%async_computation | async-start | bytes 1048576 | tf_op jit(solution)/shard_map/while/body/eval_jaxpr/all_to_all | solution.py:30
  414.7 15.5 %all-to-all-start.5 = ((f32[32,32,128]{2,1,0:T(8,128)}), f32[32,32,128]{2,1,0:T(8,128)S(1)}, u32[]{:S(2)}, u32[]{:S(2)}) async-start(f32[32,32,128]{2,1,0:T(8,128)} %broadcast_in_dim.63), calls=%async_computation.5 | async-start | bytes 1048576 | tf_op jit(solution)/shard_map/while/body/eval_jaxpr/all_to_all | solution.py:15
  434.8 15.5 %all-to-all-start.6 = ((f32[32,32,128]{2,1,0:T(8,128)}), f32[32,32,128]{2,1,0:T(8,128)S(1)}, u32[]{:S(2)}, u32[]{:S(2)}) async-start(f32[32,32,128]{2,1,0:T(8,128)} %broadcast_in_dim.64), calls=%async_computation.6 | async-start | bytes 1048576 | tf_op jit(solution)/shard_map/while/body/eval_jaxpr/all_to_all | solution.py:15
  438.8 39.3 %collective-permute-start.1 = (f32[32,128]{1,0:T(8,128)S(1)}, f32[32,128]{1,0:T(8,128)S(1)}, u32[]{:S(2)}, u32[]{:S(2)}) collective-permute-start(f32[32,128]{1,0:T(8,128)S(1)} %get-tuple-element.383), channel_id=1, source_target_pairs={{32,0},{64,32},{96,64},{33,1},{65,33},{97,65},{34,2},{66,34},{98,6... | collective-permute-start | bytes 49160 | tf_op jit(solution)/shard_map/while/body/eval_jaxpr/ppermute | solution.py:37
  454.9 15.5 %all-to-all-start.7 = ((f32[32,32,128]{2,1,0:T(8,128)}), f32[32,32,128]{2,1,0:T(8,128)S(1)}, u32[]{:S(2)}, u32[]{:S(2)}) async-start(f32[32,32,128]{2,1,0:T(8,128)} %broadcast_in_dim.65), calls=%async_computation.7 | async-start | bytes 1048576 | tf_op jit(solution)/shard_map/while/body/eval_jaxpr/all_to_all | solution.py:15
  474.1 4.8 collective-permute-start
  482.6 16.3 %all-to-all-start = ((f32[32,128,32]{1,2,0:T(8,128)}), f32[32,128,32]{1,2,0:T(8,128)S(1)}, u32[]{:S(2)}, u32[]{:S(2)}) async-start(f32[32,128,32]{1,2,0:T(8,128)} %bitcast.256), calls=%async_computation | async-start | bytes 1048576 | tf_op jit(solution)/shard_map/while/body/eval_jaxpr/all_to_all | solution.py:30
  572.5 15.5 %all-to-all-start.5 = ((f32[32,32,128]{2,1,0:T(8,128)}), f32[32,32,128]{2,1,0:T(8,128)S(1)}, u32[]{:S(2)}, u32[]{:S(2)}) async-start(f32[32,32,128]{2,1,0:T(8,128)} %broadcast_in_dim.63), calls=%async_computation.5 | async-start | bytes 1048576 | tf_op jit(solution)/shard_map/while/body/eval_jaxpr/all_to_all | solution.py:15
  592.6 15.5 %all-to-all-start.6 = ((f32[32,32,128]{2,1,0:T(8,128)}), f32[32,32,128]{2,1,0:T(8,128)S(1)}, u32[]{:S(2)}, u32[]{:S(2)}) async-start(f32[32,32,128]{2,1,0:T(8,128)} %broadcast_in_dim.64), calls=%async_computation.6 | async-start | bytes 1048576 | tf_op jit(solution)/shard_map/while/body/eval_jaxpr/all_to_all | solution.py:15
  596.6 39.3 %collective-permute-start.1 = (f32[32,128]{1,0:T(8,128)S(1)}, f32[32,128]{1,0:T(8,128)S(1)}, u32[]{:S(2)}, u32[]{:S(2)}) collective-permute-start(f32[32,128]{1,0:T(8,128)S(1)} %get-tuple-element.383), channel_id=1, source_target_pairs={{32,0},{64,32},{96,64},{33,1},{65,33},{97,65},{34,2},{66,34},{98,6... | collective-permute-start | bytes 49160 | tf_op jit(solution)/shard_map/while/body/eval_jaxpr/ppermute | solution.py:37
  612.7 15.5 %all-to-all-start.7 = ((f32[32,32,128]{2,1,0:T(8,128)}), f32[32,32,128]{2,1,0:T(8,128)S(1)}, u32[]{:S(2)}, u32[]{:S(2)}) async-start(f32[32,32,128]{2,1,0:T(8,128)} %broadcast_in_dim.65), calls=%async_computation.7 | async-start | bytes 1048576 | tf_op jit(solution)/shard_map/while/body/eval_jaxpr/all_to_all | solution.py:15
  631.9 4.8 collective-permute-start
  (10 other events, 419.9 us)
where the time goes:
time: 641 us; the launch traced here: 637 us
  blocking collectives  241 us (38%)
  waiting for transfers between devices  182 us (28%)
  matrix products  104 us (16%)
  starting transfers between devices  91.2 us (14%)
  local copies, waits for them, and re-layouts  15.6 us (2%)
    all_to_all x12, blocking collectives, summed_on_arrival(): lax.all_to_all(blocks, axis, split_axis=0, concat_axis=0, tiled=True)  181 us
    all_to_all x12, waiting for transfers between devices, copy_for_each(): return lax.all_to_all(copies, axis, split_axis=0, concat_axis=0, tiled=True)  133 us
    all_to_all x4, blocking collectives, copy_for_each(): return lax.all_to_all(copies, axis, split_axis=0, concat_axis=0, tiled=True)  60.2 us
    dot_general x16, matrix products, forward_apply(): lax.dot_general(gather_directly(source, 'cross', 1), matrix, (((1,), (1,)...  59.5 us
    all_to_all x12, starting transfers between devices, copy_for_each(): return lax.all_to_all(copies, axis, split_axis=0, concat_axis=0, tiled=True)  47.2 us
    all_to_all x4, waiting for transfers between devices, summed_on_arrival(): lax.all_to_all(blocks, axis, split_axis=0, concat_axis=0, tiled=True)  46 us
    dot_general x16, matrix products, backward_apply(): lax.dot_general(matrix, source, (((0,), (1,)), ((), ())), precision=lax.P...  44.5 us
    all_to_all x4, starting transfers between devices, summed_on_arrival(): lax.all_to_all(blocks, axis, split_axis=0, concat_axis=0, tiled=True)  23.9 us
  transfers between devices with their start and end apart: 24, of which 20 were waited for; matrix products, arithmetic and copies ran while one was open for 5% of the time, Pallas kernels for 0%

commit v1 on v0

v1 whole, which is shorter than its diff:
```python
import jax
import jax.numpy as jnp
from jax import lax
from jax.experimental import pallas as pl
from jax.experimental.pallas import tpu as pltpu
from jax.sharding import PartitionSpec as P

MESH = pl.DeviceIdType.MESH
SIDE = 4
CHIPS = SIDE * SIDE
HOPS = sorted(
    ((dz, dy) for dz in range(SIDE) for dy in range(SIDE)),
    key=lambda d: min(d[0], SIDE - d[0]) + min(d[1], SIDE - d[1]),
)
LAYERS = 4
HALF = 16
ROWS = 128
WIDE = 256
F32, BF16 = jnp.float32, jnp.bfloat16


def penalty(flag_cells):
    factor = jnp.where(flag_cells == 0, 0.98, jnp.where(flag_cells == 1, 0.05, 0.5)).astype(F32)
    return jnp.repeat(factor, 2, axis=-1)


def split_two(value):
    high = value.astype(BF16)
    return high, (value - high.astype(F32)).astype(BF16)


def permuted(value, table):
    high = value.astype(BF16)
    rest = value - high.astype(F32)
    mid = rest.astype(BF16)
    low = (rest - mid.astype(F32)).astype(BF16)
    return sum(jnp.dot(part, table, preferred_element_type=F32) for part in (high, mid, low))


def kernel(
    forcing, cotangent, factor, inverses, response, gradient,
    own, even, weights, planar_of, real_of, mixed,
    drive, sink, factors, got_f, put_b, got_b, carry, out_put, out_got,
    load_sem, even_put, even_sem, mixed_put, mixed_sem, side_put, side_sem,
    f_put, f_put_self, f_sem, b_put, b_sem, carry_put, carry_sem, out_put_sem, out_sem,
):
    x = lax.axis_index("stream")
    me = lax.axis_index("cross")
    sections = lax.axis_size("stream")
    core = lax.rem(me, 2)
    chip = me // 2
    zc, yc = chip // SIDE, lax.rem(chip, SIDE)
    partner = me + 1 - 2 * core

    def chip_at(k, sign):
        dz, dy = HOPS[k]
        return lax.rem(zc + sign * dz + SIDE, SIDE) * SIDE + lax.rem(yc + sign * dy + SIDE, SIDE)

    def wait(ref, sem):
        pltpu.make_async_copy(ref, ref, sem).wait()

    def remote(src, dst, send_sem, recv_sem, section, device):
        return pltpu.make_async_remote_copy(
            src_ref=src, dst_ref=dst, send_sem=send_sem, recv_sem=recv_sem,
            device_id={"stream": section, "cross": device}, device_id_type=MESH,
        )

    barrier = pltpu.get_barrier_semaphore()

    def greet(section, device):
        pl.semaphore_signal(
            barrier, inc=1, device_id={"stream": section, "cross": device}, device_id_type=MESH
        )

    greet(x, partner)

    @pl.loop(1, CHIPS)
    def _(o):
        greet(x, lax.rem(chip + o, CHIPS) * 2 + core)

    @pl.when(x > 0)
    def _():
        @pl.loop(0, CHIPS)
        def _(o):
            greet(x - 1, o * 2 + core)

    @pl.when(x < sections - 1)
    def _():
        @pl.loop(0, CHIPS)
        def _(o):
            greet(x + 1, o * 2 + core)

    first_forward = x < sections // 2

    def layer_of(forward, i):
        f = forward.astype(jnp.int32)
        return f * i + (1 - f) * (LAYERS - 1 - i)

    @pl.loop(0, LAYERS)
    def _(i):
        l = layer_of(first_forward, i)
        for j in range(2 * CHIPS):
            pltpu.make_async_copy(
                inverses.at[l, :, pl.ds(j * ROWS, ROWS)], own.at[l, j], load_sem.at[l]
            ).start()

    r = lax.broadcasted_iota(jnp.int32, (WIDE, WIDE), 0)
    k = lax.broadcasted_iota(jnp.int32, (WIDE, WIDE), 1)
    planar_of[...] = (r == 2 * (k % ROWS) + k // ROWS).astype(F32).astype(BF16)
    real_of[...] = (k == 2 * (r % ROWS) + r // ROWS).astype(F32).astype(BF16)
    mine = pl.ds(pl.multiple_of(HALF * core, HALF), HALF)
    theirs = pl.ds(pl.multiple_of(HALF * (1 - core), HALF), HALF)
    mixed[core, 0:4] = forcing[:, mine, :]
    mixed[core, 4:8] = cotangent[:, mine, :]
    mixed[core, 8:12] = factor[...]

    beside = (x > 0).astype(jnp.int32) + (x < sections - 1).astype(jnp.int32)
    pl.semaphore_wait(barrier, CHIPS + CHIPS * beside)

    mixed_copies = [
        remote(src, mixed.at[core, pl.ds(4 * j, 4)], mixed_put.at[j], mixed_sem.at[j], x, partner)
        for j, src in enumerate((forcing.at[:, theirs, :], cotangent.at[:, theirs, :], factor))
    ]
    for copy in mixed_copies:
        copy.start()

    @pl.loop(0, LAYERS)
    def _(i):
        l = layer_of(first_forward, i)
        wait(own.at[l], load_sem.at[l])
        for q in range(CHIPS):
            for h in range(2):
                even[l, core, q, :, h * ROWS : (h + 1) * ROWS] = own[
                    l, 2 * q + h, pl.ds(0, ROWS // 2, stride=2), :
                ]
        remote(even.at[l, core], even.at[l, core], even_put.at[l], even_sem.at[l], x, partner).start()

    for j in range(3):
        wait(mixed.at[0, pl.ds(4 * j, 4)], mixed_sem.at[j])
    tall = jnp.concatenate(
        [mixed[0].reshape(12 * HALF, ROWS), mixed[1].reshape(12 * HALF, ROWS)], axis=-1
    )
    tall = permuted(tall, planar_of[...]).reshape(12, HALF, WIDE)
    drive[0:4] = tall[0:4]
    sink[1:5] = tall[4:8]
    factors[0:4] = tall[8:12]

    def send_forward(step):
        for k in range(CHIPS - 1, 0, -1):
            remote(
                got_f.at[step, 0], got_f.at[lax.rem(step, LAYERS), k], f_put.at[step],
                f_sem.at[lax.rem(step, LAYERS), k], x + step // LAYERS, chip_at(k, 1) * 2 + core,
            ).start()

    @pl.when(x == 0)
    def _():
        got_f[0, 0] = drive[0]
        send_forward(0)

    @pl.when(x == sections - 1)
    def _():
        carry[LAYERS] = sink[LAYERS]

    @pl.when(x > 0)
    def _():
        remote(drive.at[0], drive.at[LAYERS], side_put.at[0], side_sem.at[0], x - 1, me).start()
        remote(factors.at[0], factors.at[LAYERS], side_put.at[1], side_sem.at[1], x - 1, me).start()

    @pl.when(x < sections - 1)
    def _():
        remote(sink.at[LAYERS], sink.at[0], side_put.at[2], side_sem.at[2], x + 1, me).start()

    def prepare(l):
        wait(even.at[l, core], even_sem.at[l])

        @pl.loop(0, CHIPS)
        def _(q):
            high, low = split_two(jnp.concatenate([even[l, 0, q], even[l, 1, q]], axis=0))
            both = jnp.concatenate([high, low], axis=0)
            weights[l, q] = jnp.dot(both, planar_of[...], preferred_element_type=F32).astype(BF16)

    middle = jnp.logical_and(x > 0, x < sections - 1).astype(jnp.int32)

    @pl.loop(0, 1 + (LAYERS - 1) * middle)
    def _(i):
        prepare(layer_of(first_forward, i))

    def prepare_next(phase, i, forward):
        @pl.when(jnp.logical_and(jnp.logical_and(phase == 0, middle == 0), i < LAYERS - 1))
        def _():
            prepare(layer_of(forward, i + 1))

    def put_out(kind, l, value, out):
        real = permuted(value, real_of[...])
        out_put[kind, l, 0] = real[:, :ROWS]
        out_put[kind, l, 1] = real[:, ROWS:]
        out[l, mine, :] = out_put[kind, l, core]
        remote(
            out_put.at[kind, l, 1 - core], out_got.at[kind, l], out_put_sem.at[kind, l],
            out_sem.at[kind, l], x, partner,
        ).start()

    def forward_step(phase, i):
        l = i

        @pl.when(jnp.logical_and(l == 0, x > 0))
        def _():
            wait(got_f.at[0, 0], f_sem.at[0, 0])

        total = jnp.zeros((4 * HALF, WIDE), F32)
        for k in range(CHIPS):
            if k > 0:
                wait(got_f.at[l, k], f_sem.at[l, k])
            high, low = split_two(got_f[l, k])
            left = jnp.concatenate([high, low], axis=0)
            turned = jnp.concatenate([left[:, ROWS:], -left[:, :ROWS]], axis=1)
            left = jnp.concatenate([left, turned], axis=0)
            total = total + lax.dot_general(
                left, weights[l, chip_at(k, -1)], (((1,), (1,)), ((), ())), preferred_element_type=F32
            )
        total = total[:, :ROWS] + total[:, ROWS:]
        result = jnp.concatenate(
            [total[:HALF] + total[HALF : 2 * HALF], total[2 * HALF : 3 * HALF] + total[3 * HALF :]], axis=1
        )

        @pl.when(jnp.logical_and(l == LAYERS - 1, x < sections - 1))
        def _():
            wait(drive.at[LAYERS], side_sem.at[0])
            wait(factors.at[LAYERS], side_sem.at[1])

        @pl.when(jnp.logical_or(l < LAYERS - 1, x < sections - 1))
        def _():
            got_f[l + 1, 0] = drive[l + 1] + factors[l + 1] * result
            send_forward(l + 1)

            @pl.when(l == LAYERS - 1)
            def _():
                remote(
                    got_f.at[LAYERS, 0], got_f.at[0, 0], f_put_self, f_sem.at[0, 0], x + 1, me
                ).start()

        put_out(0, l, result, response)
        prepare_next(phase, i, jnp.bool_(True))

    def backward_step(phase, i):
        l = LAYERS - 1 - i

        @pl.when(jnp.logical_and(l == LAYERS - 1, x < sections - 1))
        def _():
            wait(carry.at[LAYERS], carry_sem)

        high, low = split_two(carry[l + 1])
        column = jnp.concatenate(
            [high[:, :ROWS], high[:, ROWS:], low[:, :ROWS], low[:, ROWS:]], axis=0
        )
        left = jnp.concatenate([column, column], axis=1)
        for k in range(CHIPS - 1, -1, -1):
            to = chip_at(k, 1)
            part = jnp.dot(left, weights[l, to], preferred_element_type=F32)
            part = part[: 2 * HALF] + part[2 * HALF :]
            real, imag = part[:HALF], part[HALF:]
            part = jnp.concatenate(
                [real[:, :ROWS] - imag[:, ROWS:], real[:, ROWS:] + imag[:, :ROWS]], axis=1
            )
            if k > 0:
                put_b[l, k] = part
                remote(
                    put_b.at[l, k], got_b.at[l, k], b_put.at[l], b_sem.at[l, k], x, to * 2 + core
                ).start()
            else:
                got_b[l, 0] = part
        prepare_next(phase, i, jnp.bool_(False))
        total = got_b[l, 0]
        for k in range(1, CHIPS):
            wait(got_b.at[l, k], b_sem.at[l, k])
            total = total + got_b[l, k]

        @pl.when(jnp.logical_and(l == 0, x > 0))
        def _():
            wait(sink.at[0], side_sem.at[2])

        @pl.when(jnp.logical_or(l > 0, x > 0))
        def _():
            carry[l] = sink[l] + factors[l] * total

        @pl.when(jnp.logical_and(l == 0, x > 0))
        def _():
            remote(carry.at[0], carry.at[LAYERS], carry_put, carry_sem, x - 1, me).start()

        put_out(1, l, total, gradient)

    @pl.loop(0, 2)
    def _(phase):
        forward = (phase == 0) == first_forward

        @pl.when(forward)
        def _():
            @pl.loop(0, LAYERS)
            def _(i):
                forward_step(phase, i)

        @pl.when(jnp.logical_not(forward))
        def _():
            @pl.loop(0, LAYERS)
            def _(i):
                backward_step(phase, i)

    for j in range(3):
        wait(mixed.at[0, pl.ds(4 * j, 4)], mixed_put.at[j])

    @pl.loop(0, LAYERS)
    def _(l):
        wait(even.at[l, core], even_put.at[l])
        wait(put_b.at[l, pl.ds(1, CHIPS - 1)], b_put.at[l])

    @pl.when(x == 0)
    def _():
        wait(got_f.at[0, pl.ds(1, CHIPS - 1)], f_put.at[0])

    @pl.loop(1, LAYERS)
    def _(l):
        wait(got_f.at[0, pl.ds(1, CHIPS - 1)], f_put.at[l])

    @pl.when(x < sections - 1)
    def _():
        wait(got_f.at[0, pl.ds(1, CHIPS - 1)], f_put.at[LAYERS])
        wait(got_f.at[0, 0], f_put_self)
        wait(sink.at[0], side_put.at[2])

    @pl.when(x > 0)
    def _():
        wait(drive.at[0], side_put.at[0])
        wait(factors.at[0], side_put.at[1])
        wait(carry.at[0], carry_put)

    for kind, out in enumerate((response, gradient)):
        @pl.loop(0, LAYERS)
        def _(l):
            wait(out_got.at[kind, l], out_sem.at[kind, l])
            out[l, theirs, :] = out_got[kind, l]
            wait(out_got.at[kind, l], out_put_sem.at[kind, l])


def shards(forcing, cotangent, inverses, flags):
    factor = jnp.broadcast_to(penalty(flags)[:, None, :], (LAYERS, HALF, ROWS))
    vmem = pl.BlockSpec(memory_space=pltpu.VMEM)
    dma = pltpu.SemaphoreType.DMA
    block = (HALF, WIDE)
    return tuple(
        pl.pallas_call(
            kernel,
            out_shape=[jax.ShapeDtypeStruct(forcing.shape, F32)] * 2,
            in_specs=[vmem, vmem, vmem, pl.BlockSpec(memory_space=pl.ANY)],
            out_specs=[vmem, vmem],
            scratch_shapes=[
                pltpu.VMEM((LAYERS, 2 * CHIPS, ROWS, ROWS), F32),
                pltpu.VMEM((LAYERS, 2, CHIPS, ROWS // 2, WIDE), F32),
                pltpu.VMEM((LAYERS, CHIPS, WIDE, WIDE), BF16),
                pltpu.VMEM((WIDE, WIDE), BF16),
                pltpu.VMEM((WIDE, WIDE), BF16),
                pltpu.VMEM((2, 12, HALF, ROWS), F32),
                pltpu.VMEM((LAYERS + 1, *block), F32),
                pltpu.VMEM((LAYERS + 1, *block), F32),
                pltpu.VMEM((LAYERS + 1, *block), F32),
                pltpu.VMEM((LAYERS + 1, CHIPS, *block), F32),
                pltpu.VMEM((LAYERS, CHIPS, *block), F32),
                pltpu.VMEM((LAYERS, CHIPS, *block), F32),
                pltpu.VMEM((LAYERS + 1, *block), F32),
                pltpu.VMEM((2, LAYERS, 2, HALF, ROWS), F32),
                pltpu.VMEM((2, LAYERS, HALF, ROWS), F32),
                dma((LAYERS,)),
                dma((LAYERS,)),
                dma((LAYERS,)),
                dma((3,)),
                dma((3,)),
                dma((3,)),
                dma((3,)),
                dma((LAYERS + 1,)),
                dma,
                dma((LAYERS, CHIPS)),
                dma((LAYERS,)),
                dma((LAYERS, CHIPS)),
                dma,
                dma,
                dma((2, LAYERS)),
                dma((2, LAYERS)),
            ],
            compiler_params=pltpu.CompilerParams(
                collective_id=0, has_side_effects=True, vmem_limit_bytes=60 << 20
            ),
        )(forcing, cotangent, factor, inverses)
    )


def solution(mesh):
    in_specs = (
        P("stream", None, "cross"),
        P("stream", None, "cross"),
        P("stream", "cross", None),
        P("stream", "cross"),
    )
    out_specs = (P("stream", None, "cross"), P("stream", None, "cross"))
    return jax.shard_map(shards, mesh=mesh, in_specs=in_specs, out_specs=out_specs, check_vma=False)
```

time: 641 us -> 137 us (0.21)
  blocking collectives: 241 us -> 0 us
  waiting for transfers between devices: 182 us -> 0 us
  Pallas kernels: 0 us -> 132 us
  matrix products: 104 us -> 0 us
  starting transfers between devices: 91.2 us -> 0 us
  local copies, waits for them, and re-layouts: 15.6 us -> 3.77 us
    all_to_all x16 -> x0, blocking collectives: 241 us -> none  [the longest x12 181 us: summed_on_arrival(): lax.all_to_all(blocks, axis, split_axis=0, concat_axis=0, tiled=True)]
    all_to_all x16 -> x0, waiting for transfers between devices: 179 us -> none  [the longest x12 133 us: copy_for_each(): return lax.all_to_all(copies, axis, split_axis=0, concat_axis=0, tiled=True)]
    pallas_call x0 -> x1, Pallas kernels: none -> 132 us  [shards(): pl.pallas_call(kernel, out_shape=[jax.ShapeDtypeStruct(forcing.shape, F32...]
    dot_general x32 -> x0, matrix products: 104 us -> none  [the longest x16 59.5 us: forward_apply(): lax.dot_general(gather_directly(source, 'cross', 1), matrix, (((1,), (1,)...]
    all_to_all x16 -> x0, starting transfers between devices: 71.2 us -> none  [the longest x12 47.2 us: copy_for_each(): return lax.all_to_all(copies, axis, split_axis=0, concat_axis=0, tiled=True)]
    ppermute x8 -> x0, starting transfers between devices: 20 us -> none  [shifted(): return lax.ppermute(block, axis, route)]
    broadcast_in_dim x20 -> x2, local copies, waits for them, and re-layouts: 10.5 us -> 0.7 us  [shards(): factor = jnp.broadcast_to(penalty(flags)[:, None, :], (LAYERS, HALF, ROWS))]
  transfers between devices with their start and end apart: 24 -> 0, of which waited for: 20 -> 0; matrix products, arithmetic and copies ran while one was open for 5% -> 0% of each run, Pallas kernels for 0% -> 0%
where the time goes in v1:
time: 137 us
  Pallas kernels  132 us (96%)
  local copies, waits for them, and re-layouts  3.77 us (3%)
    pallas_call x1, Pallas kernels, shards(): pl.pallas_call(kernel, out_shape=[jax.ShapeDtypeStruct(forcing.shape, F32...  132 us
    unnamed x2, local copies, waits for them, and re-layouts  2.95 us

profile of v1, /device:TPU:1, one launch (start us, length us, event | category | flops | bytes accessed | tf_op | source)
XLA Modules:
  0.0 136.6 jit_solution(16273118592322653640)
XLA Ops:
  0.6 0.7 select_select_fusion
  1.3 0.1 copy.6
  1.4 0.1 copy.7
  1.5 0.6 broadcast_in_dim.27.factor
  2.1 131.5 %shard_map.59 = (f32[4,32,128]{2,1,0:T(8,128)}, f32[4,32,128]{2,1,0:T(8,128)}) custom-call(f32[4,32,128]{2,1,0:T(8,128)} %forcing.1, f32[4,32,128]{2,1,0:T(8,128)} %cotangent.1, f32[4,16,128]{2,1,0:T(8,128)} %broadcast_in_dim.27.factor, f32[4,128,4096]{2,1,0:T(8,128)} %inverses.1), custom_call_target="tpu_custom_call" | custom-call | tf_op jit(solution)/shard_map/pallas_call | solution.py:350
  133.7 1.5 %copy.10 = f32[4,32,128]{2,1,0:T(8,128)} copy(f32[4,32,128]{2,1,0:T(8,128)} %get-tuple-element.4) | data formatting | bytes 131072
  135.1 1.5 %copy.11 = f32[4,32,128]{2,1,0:T(8,128)} copy(f32[4,32,128]{2,1,0:T(8,128)} %get-tuple-element.5) | data formatting | bytes 131072
  (1 shorter events, 0.0 us)

commit v2 on v1

--- a/solution.py
+++ b/solution.py
@@ -12,6 +12,8 @@
     ((dz, dy) for dz in range(SIDE) for dy in range(SIDE)),
     key=lambda d: min(d[0], SIDE - d[0]) + min(d[1], SIDE - d[1]),
 )
+GROUPS = ((0,), (1, 2, 3, 4), (5, 6, 7, 8, 9, 10), (11, 12, 13, 14), (15,))
+PUSHES = ((15, 14, 13, 12, 11), (10, 9, 8, 7, 6, 5), (4, 3, 2, 1, 0))
 LAYERS = 4
 HALF = 16
 ROWS = 128
@@ -20,8 +22,7 @@
 
 
 def penalty(flag_cells):
-    factor = jnp.where(flag_cells == 0, 0.98, jnp.where(flag_cells == 1, 0.05, 0.5)).astype(F32)
-    return jnp.repeat(factor, 2, axis=-1)
+    return jnp.where(flag_cells == 0, 0.98, jnp.where(flag_cells == 1, 0.05, 0.5)).astype(F32)
 
 
 def split_two(value):
@@ -38,11 +39,11 @@
 
 
 def kernel(
-    forcing, cotangent, factor, inverses, response, gradient,
-    own, even, weights, planar_of, real_of, mixed,
-    drive, sink, factors, got_f, put_b, got_b, carry, out_put, out_got,
+    forcing, cotangent, flags, inverses, response, gradient,
+    own, even, weights, planar_of, real_of, cells, factor, mixed,
+    drive, sink, factors, got_f, put_b, got_b, carry, totals, back, out_put, out_got,
     load_sem, even_put, even_sem, mixed_put, mixed_sem, side_put, side_sem,
-    f_put, f_put_self, f_sem, b_put, b_sem, carry_put, carry_sem, out_put_sem, out_sem,
+    f_put, f_put_self, f_sem, b_put, b_put_self, b_sem, back_put, back_sem, out_put_sem, out_sem,
 ):
     x = lax.axis_index("stream")
     me = lax.axis_index("cross")
@@ -110,10 +111,28 @@
     real_of[...] = (k == 2 * (r % ROWS) + r // ROWS).astype(F32).astype(BF16)
     mine = pl.ds(pl.multiple_of(HALF * core, HALF), HALF)
     theirs = pl.ds(pl.multiple_of(HALF * (1 - core), HALF), HALF)
+    cells[...] = jnp.zeros_like(cells)
+    cells[0:LAYERS, 0 : ROWS // 2] = penalty(flags[...])
+    twice = r[:ROWS, :ROWS] == k[:ROWS, :ROWS] // 2
+    doubled = permuted(cells[...], twice.astype(F32).astype(BF16))
+    for l in range(LAYERS):
+        factor[l] = jnp.broadcast_to(doubled[l : l + 1], (HALF, ROWS))
     mixed[core, 0:4] = forcing[:, mine, :]
     mixed[core, 4:8] = cotangent[:, mine, :]
     mixed[core, 8:12] = factor[...]
 
+    def extract(l):
+        wait(own.at[l], load_sem.at[l])
+        for q in range(CHIPS):
+            for h in range(2):
+                even[l, core, q, :, h * ROWS : (h + 1) * ROWS] = own[
+                    l, 2 * q + h, pl.ds(0, ROWS // 2, stride=2), :
+                ]
+
+    def send_even(l):
+        remote(even.at[l, core], even.at[l, core], even_put.at[l], even_sem.at[l], x, partner).start()
+
+    extract(layer_of(first_forward, 0))
     beside = (x > 0).astype(jnp.int32) + (x < sections - 1).astype(jnp.int32)
     pl.semaphore_wait(barrier, CHIPS + CHIPS * beside)
 
@@ -123,27 +142,14 @@
     ]
     for copy in mixed_copies:
         copy.start()
-
-    @pl.loop(0, LAYERS)
-    def _(i):
-        l = layer_of(first_forward, i)
-        wait(own.at[l], load_sem.at[l])
-        for q in range(CHIPS):
-            for h in range(2):
-                even[l, core, q, :, h * ROWS : (h + 1) * ROWS] = own[
-                    l, 2 * q + h, pl.ds(0, ROWS // 2, stride=2), :
-                ]
-        remote(even.at[l, core], even.at[l, core], even_put.at[l], even_sem.at[l], x, partner).start()
-
-    for j in range(3):
+    send_even(layer_of(first_forward, 0))
+
+    def planar(j):
         wait(mixed.at[0, pl.ds(4 * j, 4)], mixed_sem.at[j])
-    tall = jnp.concatenate(
-        [mixed[0].reshape(12 * HALF, ROWS), mixed[1].reshape(12 * HALF, ROWS)], axis=-1
-    )
-    tall = permuted(tall, planar_of[...]).reshape(12, HALF, WIDE)
-    drive[0:4] = tall[0:4]
-    sink[1:5] = tall[4:8]
-    factors[0:4] = tall[8:12]
+        tall = jnp.concatenate(
+            [mixed[h, 4 * j : 4 * j + 4].reshape(LAYERS * HALF, ROWS) for h in range(2)], axis=-1
+        )
+        return permuted(tall, planar_of[...]).reshape(LAYERS, HALF, WIDE)
 
     def send_forward(step):
         for k in range(CHIPS - 1, 0, -1):
@@ -152,28 +158,35 @@
                 f_sem.at[lax.rem(step, LAYERS), k], x + step // LAYERS, chip_at(k, 1) * 2 + core,
             ).start()
 
+    drive[0:LAYERS] = planar(0)
+
     @pl.when(x == 0)
     def _():
         got_f[0, 0] = drive[0]
         send_forward(0)
 
+    sink[...] = planar(1)
+    factors[0:LAYERS] = planar(2)
+
     @pl.when(x == sections - 1)
     def _():
-        carry[LAYERS] = sink[LAYERS]
+        carry[...] = sink[LAYERS - 1]
+
+    @pl.loop(1, LAYERS)
+    def _(i):
+        l = layer_of(first_forward, i)
+        extract(l)
+        send_even(l)
 
     @pl.when(x > 0)
     def _():
         remote(drive.at[0], drive.at[LAYERS], side_put.at[0], side_sem.at[0], x - 1, me).start()
         remote(factors.at[0], factors.at[LAYERS], side_put.at[1], side_sem.at[1], x - 1, me).start()
 
-    @pl.when(x < sections - 1)
-    def _():
-        remote(sink.at[LAYERS], sink.at[0], side_put.at[2], side_sem.at[2], x + 1, me).start()
-
     def prepare(l):
         wait(even.at[l, core], even_sem.at[l])
 
-        @pl.loop(0, CHIPS)
+        @pl.loop(0, CHIPS, unroll=4)
         def _(q):
             high, low = split_two(jnp.concatenate([even[l, 0, q], even[l, 1, q]], axis=0))
             both = jnp.concatenate([high, low], axis=0)
@@ -200,6 +213,12 @@
             out_sem.at[kind, l], x, partner,
         ).start()
 
+    def wait_side(phase, l):
+        @pl.when(jnp.logical_and(jnp.logical_and(l == LAYERS - 1, x < sections - 1), phase == 0))
+        def _():
+            wait(drive.at[LAYERS], side_sem.at[0])
+            wait(factors.at[LAYERS], side_sem.at[1])
+
     def forward_step(phase, i):
         l = i
 
@@ -208,25 +227,24 @@
             wait(got_f.at[0, 0], f_sem.at[0, 0])
 
         total = jnp.zeros((4 * HALF, WIDE), F32)
-        for k in range(CHIPS):
-            if k > 0:
-                wait(got_f.at[l, k], f_sem.at[l, k])
-            high, low = split_two(got_f[l, k])
-            left = jnp.concatenate([high, low], axis=0)
-            turned = jnp.concatenate([left[:, ROWS:], -left[:, :ROWS]], axis=1)
-            left = jnp.concatenate([left, turned], axis=0)
-            total = total + lax.dot_general(
-                left, weights[l, chip_at(k, -1)], (((1,), (1,)), ((), ())), preferred_element_type=F32
-            )
+        for group in GROUPS:
+            for k in group:
+                if k > 0:
+                    wait(got_f.at[l, k], f_sem.at[l, k])
+            for k in group:
+                high, low = split_two(got_f[l, k])
+                left = jnp.concatenate([high, low], axis=0)
+                turned = jnp.concatenate([left[:, ROWS:], -left[:, :ROWS]], axis=1)
+                left = jnp.concatenate([left, turned], axis=0)
+                total = total + lax.dot_general(
+                    left, weights[l, chip_at(k, -1)], (((1,), (1,)), ((), ())), preferred_element_type=F32
+                )
         total = total[:, :ROWS] + total[:, ROWS:]
         result = jnp.concatenate(
             [total[:HALF] + total[HALF : 2 * HALF], total[2 * HALF : 3 * HALF] + total[3 * HALF :]], axis=1
         )
 
-        @pl.when(jnp.logical_and(l == LAYERS - 1, x < sections - 1))
-        def _():
-            wait(drive.at[LAYERS], side_sem.at[0])
-            wait(factors.at[LAYERS], side_sem.at[1])
+        wait_side(phase, l)
 
         @pl.when(jnp.logical_or(l < LAYERS - 1, x < sections - 1))
         def _():
@@ -242,52 +260,73 @@
         put_out(0, l, result, response)
         prepare_next(phase, i, jnp.bool_(True))
 
+    def summed(slot):
+        total = got_b[slot, 0]
+        for group in GROUPS[1:]:
+            for k in group:
+                wait(got_b.at[slot, k], b_sem.at[slot, k])
+            for k in group:
+                total = total + got_b[slot, k]
+        return total
+
     def backward_step(phase, i):
         l = LAYERS - 1 - i
 
-        @pl.when(jnp.logical_and(l == LAYERS - 1, x < sections - 1))
-        def _():
-            wait(carry.at[LAYERS], carry_sem)
-
-        high, low = split_two(carry[l + 1])
+        last = l == LAYERS - 1
+        inner = l < LAYERS - 1
+        wait_side(phase, l)
+
+        @pl.when(jnp.logical_or(inner, x < sections - 1))
+        def _():
+            @pl.when(last)
+            def _():
+                wait(got_b.at[LAYERS, 0], b_sem.at[LAYERS, 0])
+
+            total = summed(l + 1)
+            totals[l + 1] = total
+            carry[...] = sink[l] + factors[l + 1] * total
+
+        high, low = split_two(carry[...])
         column = jnp.concatenate(
             [high[:, :ROWS], high[:, ROWS:], low[:, :ROWS], low[:, ROWS:]], axis=0
         )
         left = jnp.concatenate([column, column], axis=1)
-        for k in range(CHIPS - 1, -1, -1):
-            to = chip_at(k, 1)
-            part = jnp.dot(left, weights[l, to], preferred_element_type=F32)
-            part = part[: 2 * HALF] + part[2 * HALF :]
-            real, imag = part[:HALF], part[HALF:]
-            part = jnp.concatenate(
-                [real[:, :ROWS] - imag[:, ROWS:], real[:, ROWS:] + imag[:, :ROWS]], axis=1
-            )
-            if k > 0:
-                put_b[l, k] = part
-                remote(
-                    put_b.at[l, k], got_b.at[l, k], b_put.at[l], b_sem.at[l, k], x, to * 2 + core
-                ).start()
-            else:
-                got_b[l, 0] = part
+        leaves = jnp.logical_and(l == 0, x > 0).astype(jnp.int32)
+        slot = l + LAYERS * leaves
+        for group in PUSHES:
+            for k in group:
+                part = jnp.dot(left, weights[l, chip_at(k, 1)], preferred_element_type=F32)
+                part = part[: 2 * HALF] + part[2 * HALF :]
+                real, imag = part[:HALF], part[HALF:]
+                put_b[l, k] = jnp.concatenate(
+                    [real[:, :ROWS] - imag[:, ROWS:], real[:, ROWS:] + imag[:, :ROWS]], axis=1
+                )
+            for k in group:
+                if k > 0:
+                    remote(
+                        put_b.at[l, k], got_b.at[slot, k], b_put.at[l], b_sem.at[slot, k],
+                        x - leaves, chip_at(k, 1) * 2 + core,
+                    ).start()
+
+        @pl.when(leaves > 0)
+        def _():
+            remote(
+                put_b.at[l, 0], got_b.at[LAYERS, 0], b_put_self, b_sem.at[LAYERS, 0], x - 1, me
+            ).start()
+
+        @pl.when(leaves == 0)
+        def _():
+            got_b[l, 0] = put_b[l, 0]
+
         prepare_next(phase, i, jnp.bool_(False))
-        total = got_b[l, 0]
-        for k in range(1, CHIPS):
-            wait(got_b.at[l, k], b_sem.at[l, k])
-            total = total + got_b[l, k]
-
-        @pl.when(jnp.logical_and(l == 0, x > 0))
-        def _():
-            wait(sink.at[0], side_sem.at[2])
-
-        @pl.when(jnp.logical_or(l > 0, x > 0))
-        def _():
-            carry[l] = sink[l] + factors[l] * total
-
-        @pl.when(jnp.logical_and(l == 0, x > 0))
-        def _():
-            remote(carry.at[0], carry.at[LAYERS], carry_put, carry_sem, x - 1, me).start()
-
-        put_out(1, l, total, gradient)
+
+        @pl.when(inner)
+        def _():
+            put_out(1, l + 1, totals[l + 1], gradient)
+
+        @pl.when(jnp.logical_and(last, x < sections - 1))
+        def _():
+            remote(totals.at[LAYERS], back, back_put, back_sem, x + 1, me).start()
 
     @pl.loop(0, 2)
     def _(phase):
@@ -305,6 +344,15 @@
             def _(i):
                 backward_step(phase, i)
 
+    @pl.when(x == 0)
+    def _():
+        back[...] = summed(0)
+
+    @pl.when(x > 0)
+    def _():
+        wait(back, back_sem)
+
+    put_out(1, 0, back[...], gradient)
     for j in range(3):
         wait(mixed.at[0, pl.ds(4 * j, 4)], mixed_put.at[j])
 
@@ -325,13 +373,13 @@
     def _():
         wait(got_f.at[0, pl.ds(1, CHIPS - 1)], f_put.at[LAYERS])
         wait(got_f.at[0, 0], f_put_self)
-        wait(sink.at[0], side_put.at[2])
+        wait(back, back_put)
 
     @pl.when(x > 0)
     def _():
         wait(drive.at[0], side_put.at[0])
         wait(factors.at[0], side_put.at[1])
-        wait(carry.at[0], carry_put)
+        wait(carry, b_put_self)
 
     for kind, out in enumerate((response, gradient)):
         @pl.loop(0, LAYERS)
@@ -342,7 +390,6 @@
 
 
 def shards(forcing, cotangent, inverses, flags):
-    factor = jnp.broadcast_to(penalty(flags)[:, None, :], (LAYERS, HALF, ROWS))
     vmem = pl.BlockSpec(memory_space=pltpu.VMEM)
     dma = pltpu.SemaphoreType.DMA
     block = (HALF, WIDE)
@@ -358,14 +405,18 @@
                 pltpu.VMEM((LAYERS, CHIPS, WIDE, WIDE), BF16),
                 pltpu.VMEM((WIDE, WIDE), BF16),
                 pltpu.VMEM((WIDE, WIDE), BF16),
+                pltpu.VMEM((8, ROWS), F32),
+                pltpu.VMEM((LAYERS, HALF, ROWS), F32),
                 pltpu.VMEM((2, 12, HALF, ROWS), F32),
                 pltpu.VMEM((LAYERS + 1, *block), F32),
-                pltpu.VMEM((LAYERS + 1, *block), F32),
+                pltpu.VMEM((LAYERS, *block), F32),
                 pltpu.VMEM((LAYERS + 1, *block), F32),
                 pltpu.VMEM((LAYERS + 1, CHIPS, *block), F32),
                 pltpu.VMEM((LAYERS, CHIPS, *block), F32),
-                pltpu.VMEM((LAYERS, CHIPS, *block), F32),
+                pltpu.VMEM((LAYERS + 1, CHIPS, *block), F32),
+                pltpu.VMEM(block, F32),
                 pltpu.VMEM((LAYERS + 1, *block), F32),
+                pltpu.VMEM(block, F32),
                 pltpu.VMEM((2, LAYERS, 2, HALF, ROWS), F32),
                 pltpu.VMEM((2, LAYERS, HALF, ROWS), F32),
                 dma((LAYERS,)),
@@ -373,13 +424,14 @@
                 dma((LAYERS,)),
                 dma((3,)),
                 dma((3,)),
-                dma((3,)),
-                dma((3,)),
+                dma((2,)),
+                dma((2,)),
                 dma((LAYERS + 1,)),
                 dma,
                 dma((LAYERS, CHIPS)),
                 dma((LAYERS,)),
-                dma((LAYERS, CHIPS)),
+                dma,
+                dma((LAYERS + 1, CHIPS)),
                 dma,
                 dma,
                 dma((2, LAYERS)),
@@ -388,7 +440,7 @@
             compiler_params=pltpu.CompilerParams(
                 collective_id=0, has_side_effects=True, vmem_limit_bytes=60 << 20
             ),
-        )(forcing, cotangent, factor, inverses)
+        )(forcing, cotangent, flags, inverses)
     )
 
 

time: 137 us -> 120 us (0.88)
  the two profiles are of different devices: /device:TPU:1 before, /device:TPU:7 now
where the time goes in v2:
time: 120 us
  Pallas kernels  116 us (97%)
  local copies, waits for them, and re-layouts  2.95 us (2%)
    pallas_call x1, Pallas kernels, shards(): pl.pallas_call(kernel, out_shape=[jax.ShapeDtypeStruct(forcing.shape, F32...  116 us
    unnamed x2, local copies, waits for them, and re-layouts  2.95 us

profile of v2, /device:TPU:7, one launch (start us, length us, event | category | flops | bytes accessed | tf_op | source)
XLA Modules:
  0.0 120.0 jit_solution(5081359120032584705)
XLA Ops:
  0.6 116.4 %shard_map.59 = (f32[4,32,128]{2,1,0:T(8,128)}, f32[4,32,128]{2,1,0:T(8,128)}) custom-call(f32[4,32,128]{2,1,0:T(8,128)} %forcing.1, f32[4,32,128]{2,1,0:T(8,128)} %cotangent.1, s32[4,64]{1,0:T(4,128)} %flags.1, f32[4,128,4096]{2,1,0:T(8,128)} %inverses.1), custom_call_target="tpu_custom_call" | custom-call | tf_op jit(solution)/shard_map/pallas_call | solution.py:397
  117.0 1.5 %copy.8 = f32[4,32,128]{2,1,0:T(8,128)} copy(f32[4,32,128]{2,1,0:T(8,128)} %get-tuple-element.4) | data formatting | bytes 131072
  118.5 1.5 %copy.9 = f32[4,32,128]{2,1,0:T(8,128)} copy(f32[4,32,128]{2,1,0:T(8,128)} %get-tuple-element.5) | data formatting | bytes 131072

commit v3 on v2

--- a/solution.py
+++ b/solution.py
@@ -16,6 +16,8 @@
 PUSHES = ((15, 14, 13, 12, 11), (10, 9, 8, 7, 6, 5), (4, 3, 2, 1, 0))
 LAYERS = 4
 HALF = 16
+SETS = 2
+PART = HALF // SETS
 ROWS = 128
 WIDE = 256
 F32, BF16 = jnp.float32, jnp.bfloat16
@@ -39,7 +41,8 @@
 
 
 def kernel(
-    forcing, cotangent, flags, inverses, response, gradient,
+    forcing_in, cotangent_in, flags_in, inverses, response, gradient,
+    forcing, cotangent, flags, in_sem,
     own, even, weights, planar_of, real_of, cells, factor, mixed,
     drive, sink, factors, got_f, put_b, got_b, carry, totals, back, out_put, out_got,
     load_sem, even_put, even_sem, mixed_put, mixed_sem, side_put, side_sem,
@@ -92,6 +95,9 @@
             greet(x + 1, o * 2 + core)
 
     first_forward = x < sections // 2
+    inputs = ((forcing_in, forcing), (cotangent_in, cotangent), (flags_in, flags))
+    for j, (src, dst) in enumerate(inputs):
+        pltpu.make_async_copy(src, dst, in_sem.at[j]).start()
 
     def layer_of(forward, i):
         f = forward.astype(jnp.int32)
@@ -111,6 +117,8 @@
     real_of[...] = (k == 2 * (r % ROWS) + r // ROWS).astype(F32).astype(BF16)
     mine = pl.ds(pl.multiple_of(HALF * core, HALF), HALF)
     theirs = pl.ds(pl.multiple_of(HALF * (1 - core), HALF), HALF)
+    for j, (src, dst) in enumerate(inputs):
+        pltpu.make_async_copy(src, dst, in_sem.at[j]).wait()
     cells[...] = jnp.zeros_like(cells)
     cells[0:LAYERS, 0 : ROWS // 2] = penalty(flags[...])
     twice = r[:ROWS, :ROWS] == k[:ROWS, :ROWS] // 2
@@ -151,19 +159,24 @@
         )
         return permuted(tall, planar_of[...]).reshape(LAYERS, HALF, WIDE)
 
-    def send_forward(step):
+    def rows_of(g):
+        return slice(g * PART, (g + 1) * PART)
+
+    def send_forward(step, g):
+        slot = lax.rem(step, LAYERS)
         for k in range(CHIPS - 1, 0, -1):
             remote(
-                got_f.at[step, 0], got_f.at[lax.rem(step, LAYERS), k], f_put.at[step],
-                f_sem.at[lax.rem(step, LAYERS), k], x + step // LAYERS, chip_at(k, 1) * 2 + core,
+                got_f.at[step, g, 0], got_f.at[slot, g, k], f_put.at[step, g],
+                f_sem.at[slot, g, k], x + step // LAYERS, chip_at(k, 1) * 2 + core,
             ).start()
 
     drive[0:LAYERS] = planar(0)
 
     @pl.when(x == 0)
     def _():
-        got_f[0, 0] = drive[0]
-        send_forward(0)
+        for g in range(SETS):
+            got_f[0, g, 0] = drive[0, rows_of(g)]
+            send_forward(0, g)
 
     sink[...] = planar(1)
     factors[0:LAYERS] = planar(2)
@@ -219,76 +232,71 @@
             wait(drive.at[LAYERS], side_sem.at[0])
             wait(factors.at[LAYERS], side_sem.at[1])
 
-    def forward_step(phase, i):
-        l = i
-
+    def forward_set(l, g):
         @pl.when(jnp.logical_and(l == 0, x > 0))
         def _():
-            wait(got_f.at[0, 0], f_sem.at[0, 0])
-
-        total = jnp.zeros((4 * HALF, WIDE), F32)
+            wait(got_f.at[0, g, 0], f_sem.at[0, g, 0])
+
+        total = jnp.zeros((4 * PART, WIDE), F32)
         for group in GROUPS:
             for k in group:
                 if k > 0:
-                    wait(got_f.at[l, k], f_sem.at[l, k])
-            for k in group:
-                high, low = split_two(got_f[l, k])
-                left = jnp.concatenate([high, low], axis=0)
-                turned = jnp.concatenate([left[:, ROWS:], -left[:, :ROWS]], axis=1)
-                left = jnp.concatenate([left, turned], axis=0)
+                    wait(got_f.at[l, g, k], f_sem.at[l, g, k])
+            for k in group:
+                value = got_f[l, g, k]
+                turned = jnp.concatenate([value[:, ROWS:], -value[:, :ROWS]], axis=1)
+                left = jnp.concatenate(split_two(jnp.concatenate([value, turned], axis=0)), axis=0)
                 total = total + lax.dot_general(
                     left, weights[l, chip_at(k, -1)], (((1,), (1,)), ((), ())), preferred_element_type=F32
                 )
+        total = total[: 2 * PART] + total[2 * PART :]
         total = total[:, :ROWS] + total[:, ROWS:]
-        result = jnp.concatenate(
-            [total[:HALF] + total[HALF : 2 * HALF], total[2 * HALF : 3 * HALF] + total[3 * HALF :]], axis=1
-        )
-
-        wait_side(phase, l)
+        result = jnp.concatenate([total[:PART], total[PART:]], axis=1)
 
         @pl.when(jnp.logical_or(l < LAYERS - 1, x < sections - 1))
         def _():
-            got_f[l + 1, 0] = drive[l + 1] + factors[l + 1] * result
-            send_forward(l + 1)
+            got_f[l + 1, g, 0] = drive[l + 1, rows_of(g)] + factors[l + 1, rows_of(g)] * result
+            send_forward(l + 1, g)
 
             @pl.when(l == LAYERS - 1)
             def _():
                 remote(
-                    got_f.at[LAYERS, 0], got_f.at[0, 0], f_put_self, f_sem.at[0, 0], x + 1, me
+                    got_f.at[LAYERS, g, 0], got_f.at[0, g, 0], f_put_self.at[g], f_sem.at[0, g, 0],
+                    x + 1, me,
                 ).start()
 
+        return result
+
+    def forward_step(phase, i):
+        l = i
+        wait_side(phase, l)
+        result = jnp.concatenate([forward_set(l, g) for g in range(SETS)], axis=0)
         put_out(0, l, result, response)
         prepare_next(phase, i, jnp.bool_(True))
 
-    def summed(slot):
-        total = got_b[slot, 0]
+    def summed(slot, g):
+        total = got_b[slot, g, 0]
         for group in GROUPS[1:]:
             for k in group:
-                wait(got_b.at[slot, k], b_sem.at[slot, k])
-            for k in group:
-                total = total + got_b[slot, k]
+                wait(got_b.at[slot, g, k], b_sem.at[slot, g, k])
+            for k in group:
+                total = total + got_b[slot, g, k]
         return total
 
-    def backward_step(phase, i):
-        l = LAYERS - 1 - i
-
-        last = l == LAYERS - 1
-        inner = l < LAYERS - 1
-        wait_side(phase, l)
-
-        @pl.when(jnp.logical_or(inner, x < sections - 1))
-        def _():
-            @pl.when(last)
+    def backward_set(l, g):
+        @pl.when(jnp.logical_or(l < LAYERS - 1, x < sections - 1))
+        def _():
+            @pl.when(l == LAYERS - 1)
             def _():
-                wait(got_b.at[LAYERS, 0], b_sem.at[LAYERS, 0])
-
-            total = summed(l + 1)
-            totals[l + 1] = total
-            carry[...] = sink[l] + factors[l + 1] * total
-
-        high, low = split_two(carry[...])
+                wait(got_b.at[LAYERS, g, 0], b_sem.at[LAYERS, g, 0])
+
+            total = summed(l + 1, g)
+            totals[l + 1, rows_of(g)] = total
+            carry[rows_of(g)] = sink[l, rows_of(g)] + factors[l + 1, rows_of(g)] * total
+
+        value = carry[rows_of(g)]
         column = jnp.concatenate(
-            [high[:, :ROWS], high[:, ROWS:], low[:, :ROWS], low[:, ROWS:]], axis=0
+            split_two(jnp.concatenate([value[:, :ROWS], value[:, ROWS:]], axis=0)), axis=0
         )
         left = jnp.concatenate([column, column], axis=1)
         leaves = jnp.logical_and(l == 0, x > 0).astype(jnp.int32)
@@ -296,37 +304,44 @@
         for group in PUSHES:
             for k in group:
                 part = jnp.dot(left, weights[l, chip_at(k, 1)], preferred_element_type=F32)
-                part = part[: 2 * HALF] + part[2 * HALF :]
-                real, imag = part[:HALF], part[HALF:]
-                put_b[l, k] = jnp.concatenate(
+                part = part[: 2 * PART] + part[2 * PART :]
+                real, imag = part[:PART], part[PART:]
+                put_b[l, g, k] = jnp.concatenate(
                     [real[:, :ROWS] - imag[:, ROWS:], real[:, ROWS:] + imag[:, :ROWS]], axis=1
                 )
             for k in group:
                 if k > 0:
                     remote(
-                        put_b.at[l, k], got_b.at[slot, k], b_put.at[l], b_sem.at[slot, k],
+                        put_b.at[l, g, k], got_b.at[slot, g, k], b_put.at[l, g], b_sem.at[slot, g, k],
                         x - leaves, chip_at(k, 1) * 2 + core,
                     ).start()
 
         @pl.when(leaves > 0)
         def _():
             remote(
-                put_b.at[l, 0], got_b.at[LAYERS, 0], b_put_self, b_sem.at[LAYERS, 0], x - 1, me
+                put_b.at[l, g, 0], got_b.at[LAYERS, g, 0], b_put_self.at[g], b_sem.at[LAYERS, g, 0],
+                x - 1, me,
             ).start()
 
         @pl.when(leaves == 0)
         def _():
-            got_b[l, 0] = put_b[l, 0]
+            got_b[l, g, 0] = put_b[l, g, 0]
+
+    def backward_step(phase, i):
+        l = LAYERS - 1 - i
+        wait_side(phase, l)
+        for g in range(SETS):
+            backward_set(l, g)
+
+        @pl.when(l < LAYERS - 1)
+        def _():
+            put_out(1, l + 1, totals[l + 1], gradient)
+
+        @pl.when(jnp.logical_and(l == LAYERS - 1, x < sections - 1))
+        def _():
+            remote(totals.at[LAYERS], back, back_put, back_sem, x + 1, me).start()
 
         prepare_next(phase, i, jnp.bool_(False))
-
-        @pl.when(inner)
-        def _():
-            put_out(1, l + 1, totals[l + 1], gradient)
-
-        @pl.when(jnp.logical_and(last, x < sections - 1))
-        def _():
-            remote(totals.at[LAYERS], back, back_put, back_sem, x + 1, me).start()
 
     @pl.loop(0, 2)
     def _(phase):
@@ -346,7 +361,8 @@
 
     @pl.when(x == 0)
     def _():
-        back[...] = summed(0)
+        for g in range(SETS):
+            back[rows_of(g)] = summed(0, g)
 
     @pl.when(x > 0)
     def _():
@@ -359,27 +375,37 @@
     @pl.loop(0, LAYERS)
     def _(l):
         wait(even.at[l, core], even_put.at[l])
-        wait(put_b.at[l, pl.ds(1, CHIPS - 1)], b_put.at[l])
-
-    @pl.when(x == 0)
-    def _():
-        wait(got_f.at[0, pl.ds(1, CHIPS - 1)], f_put.at[0])
-
-    @pl.loop(1, LAYERS)
-    def _(l):
-        wait(got_f.at[0, pl.ds(1, CHIPS - 1)], f_put.at[l])
+        for g in range(SETS):
+            wait(put_b.at[l, g, pl.ds(1, CHIPS - 1)], b_put.at[l, g])
+
+    for g in range(SETS):
+        sent = got_f.at[0, g, pl.ds(1, CHIPS - 1)]
+
+        @pl.when(x == 0)
+        def _():
+            wait(sent, f_put.at[0, g])
+
+        @pl.loop(1, LAYERS)
+        def _(l):
+            wait(sent, f_put.at[l, g])
+
+        @pl.when(x < sections - 1)
+        def _():
+            wait(sent, f_put.at[LAYERS, g])
+            wait(got_f.at[0, g, 0], f_put_self.at[g])
+
+        @pl.when(x > 0)
+        def _():
+            wait(got_b.at[0, g, 0], b_put_self.at[g])
 
     @pl.when(x < sections - 1)
     def _():
-        wait(got_f.at[0, pl.ds(1, CHIPS - 1)], f_put.at[LAYERS])
-        wait(got_f.at[0, 0], f_put_self)
         wait(back, back_put)
 
     @pl.when(x > 0)
     def _():
         wait(drive.at[0], side_put.at[0])
         wait(factors.at[0], side_put.at[1])
-        wait(carry, b_put_self)
 
     for kind, out in enumerate((response, gradient)):
         @pl.loop(0, LAYERS)
@@ -397,9 +423,13 @@
         pl.pallas_call(
             kernel,
             out_shape=[jax.ShapeDtypeStruct(forcing.shape, F32)] * 2,
-            in_specs=[vmem, vmem, vmem, pl.BlockSpec(memory_space=pl.ANY)],
+            in_specs=[pl.BlockSpec(memory_space=pl.ANY)] * 4,
             out_specs=[vmem, vmem],
             scratch_shapes=[
+                pltpu.VMEM((LAYERS, 2 * HALF, ROWS), F32),
+                pltpu.VMEM((LAYERS, 2 * HALF, ROWS), F32),
+                pltpu.VMEM((LAYERS, ROWS // 2), jnp.int32),
+                dma((3,)),
                 pltpu.VMEM((LAYERS, 2 * CHIPS, ROWS, ROWS), F32),
                 pltpu.VMEM((LAYERS, 2, CHIPS, ROWS // 2, WIDE), F32),
                 pltpu.VMEM((LAYERS, CHIPS, WIDE, WIDE), BF16),
@@ -411,9 +441,9 @@
                 pltpu.VMEM((LAYERS + 1, *block), F32),
                 pltpu.VMEM((LAYERS, *block), F32),
                 pltpu.VMEM((LAYERS + 1, *block), F32),
-                pltpu.VMEM((LAYERS + 1, CHIPS, *block), F32),
-                pltpu.VMEM((LAYERS, CHIPS, *block), F32),
-                pltpu.VMEM((LAYERS + 1, CHIPS, *block), F32),
+                pltpu.VMEM((LAYERS + 1, SETS, CHIPS, PART, WIDE), F32),
+                pltpu.VMEM((LAYERS, SETS, CHIPS, PART, WIDE), F32),
+                pltpu.VMEM((LAYERS + 1, SETS, CHIPS, PART, WIDE), F32),
                 pltpu.VMEM(block, F32),
                 pltpu.VMEM((LAYERS + 1, *block), F32),
                 pltpu.VMEM(block, F32),
@@ -426,19 +456,19 @@
                 dma((3,)),
                 dma((2,)),
                 dma((2,)),
-                dma((LAYERS + 1,)),
-                dma,
-                dma((LAYERS, CHIPS)),
-                dma((LAYERS,)),
-                dma,
-                dma((LAYERS + 1, CHIPS)),
+                dma((LAYERS + 1, SETS)),
+                dma((SETS,)),
+                dma((LAYERS, SETS, CHIPS)),
+                dma((LAYERS, SETS)),
+                dma((SETS,)),
+                dma((LAYERS + 1, SETS, CHIPS)),
                 dma,
                 dma,
                 dma((2, LAYERS)),
                 dma((2, LAYERS)),
             ],
             compiler_params=pltpu.CompilerParams(
-                collective_id=0, has_side_effects=True, vmem_limit_bytes=60 << 20
+                collective_id=0, has_side_effects=True, vmem_limit_bytes=57 << 20
             ),
         )(forcing, cotangent, flags, inverses)
     )

time: 120 us -> 113 us (0.942)
  the two profiles are of different devices: /device:TPU:7 before, /device:TPU:1 now
where the time goes in v3:
time: 113 us; the launch traced here: 112 us
  Pallas kernels  108 us (96%)
  local copies, waits for them, and re-layouts  2.95 us (3%)
    pallas_call x1, Pallas kernels, shards(): pl.pallas_call(kernel, out_shape=[jax.ShapeDtypeStruct(forcing.shape, F32...  108 us
    unnamed x2, local copies, waits for them, and re-layouts  2.95 us

profile of v3, /device:TPU:1, one launch (start us, length us, event | category | flops | bytes accessed | tf_op | source)
XLA Modules:
  0.0 111.6 jit_solution(3449182752544374626)
XLA Ops:
  0.6 108.0 %shard_map.59 = (f32[4,32,128]{2,1,0:T(8,128)}, f32[4,32,128]{2,1,0:T(8,128)}) custom-call(f32[4,32,128]{2,1,0:T(8,128)} %forcing_in.1, f32[4,32,128]{2,1,0:T(8,128)} %cotangent_in.1, s32[4,64]{1,0:T(4,128)} %flags_in.1, f32[4,128,4096]{2,1,0:T(8,128)} %inverses.1), custom_call_target="tpu_custom_call" | custom-call | tf_op jit(solution)/shard_map/pallas_call | solution.py:423
  108.7 1.5 %copy.8 = f32[4,32,128]{2,1,0:T(8,128)} copy(f32[4,32,128]{2,1,0:T(8,128)} %get-tuple-element.4) | data formatting | bytes 131072
  110.1 1.5 %copy.9 = f32[4,32,128]{2,1,0:T(8,128)} copy(f32[4,32,128]{2,1,0:T(8,128)} %get-tuple-element.5) | data formatting | bytes 131072

commit v4 on v3

--- a/solution.py
+++ b/solution.py
@@ -13,8 +13,9 @@
     key=lambda d: min(d[0], SIDE - d[0]) + min(d[1], SIDE - d[1]),
 )
 GROUPS = ((0,), (1, 2, 3, 4), (5, 6, 7, 8, 9, 10), (11, 12, 13, 14), (15,))
-PUSHES = ((15, 14, 13, 12, 11), (10, 9, 8, 7, 6, 5), (4, 3, 2, 1, 0))
+PUSHES = ((15, 14, 13, 12, 11), (4, 3, 2, 1, 0), (10, 9, 8, 7, 6, 5))
 LAYERS = 4
+PIECES = CHIPS // SIDE
 HALF = 16
 SETS = 2
 PART = HALF // SETS
@@ -46,7 +47,7 @@
     own, even, weights, planar_of, real_of, cells, factor, mixed,
     drive, sink, factors, got_f, put_b, got_b, carry, totals, back, out_put, out_got,
     load_sem, even_put, even_sem, mixed_put, mixed_sem, side_put, side_sem,
-    f_put, f_put_self, f_sem, b_put, b_put_self, b_sem, back_put, back_sem, out_put_sem, out_sem,
+    next_ready, last_ready, f_put, f_put_self, f_sem, b_put, b_put_self, b_sem, back_put, back_sem, out_put_sem, out_sem,
 ):
     x = lax.axis_index("stream")
     me = lax.axis_index("cross")
@@ -84,15 +85,11 @@
 
     @pl.when(x > 0)
     def _():
-        @pl.loop(0, CHIPS)
-        def _(o):
-            greet(x - 1, o * 2 + core)
+        greet(x - 1, me)
 
     @pl.when(x < sections - 1)
     def _():
-        @pl.loop(0, CHIPS)
-        def _(o):
-            greet(x + 1, o * 2 + core)
+        greet(x + 1, me)
 
     first_forward = x < sections // 2
     inputs = ((forcing_in, forcing), (cotangent_in, cotangent), (flags_in, flags))
@@ -138,11 +135,13 @@
                 ]
 
     def send_even(l):
-        remote(even.at[l, core], even.at[l, core], even_put.at[l], even_sem.at[l], x, partner).start()
+        for p in range(PIECES):
+            piece = even.at[l, core, pl.ds(p * SIDE, SIDE)]
+            remote(piece, piece, even_put.at[l], even_sem.at[l, p], x, partner).start()
 
     extract(layer_of(first_forward, 0))
     beside = (x > 0).astype(jnp.int32) + (x < sections - 1).astype(jnp.int32)
-    pl.semaphore_wait(barrier, CHIPS + CHIPS * beside)
+    pl.semaphore_wait(barrier, CHIPS + beside)
 
     mixed_copies = [
         remote(src, mixed.at[core, pl.ds(4 * j, 4)], mixed_put.at[j], mixed_sem.at[j], x, partner)
@@ -150,7 +149,20 @@
     ]
     for copy in mixed_copies:
         copy.start()
+
     send_even(layer_of(first_forward, 0))
+
+    @pl.when(x > 0)
+    def _():
+        pl.semaphore_signal(
+            next_ready, inc=1, device_id={"stream": x - 1, "cross": me}, device_id_type=MESH
+        )
+
+    @pl.when(x < sections - 1)
+    def _():
+        pl.semaphore_signal(
+            last_ready, inc=1, device_id={"stream": x + 1, "cross": me}, device_id_type=MESH
+        )
 
     def planar(j):
         wait(mixed.at[0, pl.ds(4 * j, 4)], mixed_sem.at[j])
@@ -178,36 +190,39 @@
             got_f[0, g, 0] = drive[0, rows_of(g)]
             send_forward(0, g)
 
+    def prepare(l):
+        @pl.loop(0, PIECES)
+        def _(p):
+            wait(even.at[l, core, pl.ds(p * SIDE, SIDE)], even_sem.at[l, p])
+            for j in range(SIDE):
+                q = p * SIDE + j
+                high, low = split_two(jnp.concatenate([even[l, 0, q], even[l, 1, q]], axis=0))
+                both = jnp.concatenate([high, low], axis=0)
+                weights[l, q] = jnp.dot(both, planar_of[...], preferred_element_type=F32).astype(BF16)
+
     sink[...] = planar(1)
-    factors[0:LAYERS] = planar(2)
 
     @pl.when(x == sections - 1)
     def _():
         carry[...] = sink[LAYERS - 1]
+
+    middle = jnp.logical_and(x > 0, x < sections - 1).astype(jnp.int32)
+
+    prepare(layer_of(first_forward, 0))
 
     @pl.loop(1, LAYERS)
     def _(i):
-        l = layer_of(first_forward, i)
-        extract(l)
-        send_even(l)
+        extract(layer_of(first_forward, i))
+        send_even(layer_of(first_forward, i))
+
+    factors[0:LAYERS] = planar(2)
 
     @pl.when(x > 0)
     def _():
         remote(drive.at[0], drive.at[LAYERS], side_put.at[0], side_sem.at[0], x - 1, me).start()
         remote(factors.at[0], factors.at[LAYERS], side_put.at[1], side_sem.at[1], x - 1, me).start()
 
-    def prepare(l):
-        wait(even.at[l, core], even_sem.at[l])
-
-        @pl.loop(0, CHIPS, unroll=4)
-        def _(q):
-            high, low = split_two(jnp.concatenate([even[l, 0, q], even[l, 1, q]], axis=0))
-            both = jnp.concatenate([high, low], axis=0)
-            weights[l, q] = jnp.dot(both, planar_of[...], preferred_element_type=F32).astype(BF16)
-
-    middle = jnp.logical_and(x > 0, x < sections - 1).astype(jnp.int32)
-
-    @pl.loop(0, 1 + (LAYERS - 1) * middle)
+    @pl.loop(1, 1 + (LAYERS - 1) * middle)
     def _(i):
         prepare(layer_of(first_forward, i))
 
@@ -270,6 +285,11 @@
     def forward_step(phase, i):
         l = i
         wait_side(phase, l)
+
+        @pl.when(jnp.logical_and(l == LAYERS - 1, x < sections - 1))
+        def _():
+            pl.semaphore_wait(next_ready, 1)
+
         result = jnp.concatenate([forward_set(l, g) for g in range(SETS)], axis=0)
         put_out(0, l, result, response)
         prepare_next(phase, i, jnp.bool_(True))
@@ -330,6 +350,11 @@
     def backward_step(phase, i):
         l = LAYERS - 1 - i
         wait_side(phase, l)
+
+        @pl.when(jnp.logical_and(l == 0, x > 0))
+        def _():
+            pl.semaphore_wait(last_ready, 1)
+
         for g in range(SETS):
             backward_set(l, g)
 
@@ -415,11 +440,16 @@
             wait(out_got.at[kind, l], out_put_sem.at[kind, l])
 
 
+def finish(response_in, gradient_in, response, gradient):
+    response[...] = response_in[...]
+    gradient[...] = gradient_in[...]
+
+
 def shards(forcing, cotangent, inverses, flags):
     vmem = pl.BlockSpec(memory_space=pltpu.VMEM)
     dma = pltpu.SemaphoreType.DMA
     block = (HALF, WIDE)
-    return tuple(
+    results = tuple(
         pl.pallas_call(
             kernel,
             out_shape=[jax.ShapeDtypeStruct(forcing.shape, F32)] * 2,
@@ -451,11 +481,13 @@
                 pltpu.VMEM((2, LAYERS, HALF, ROWS), F32),
                 dma((LAYERS,)),
                 dma((LAYERS,)),
-                dma((LAYERS,)),
+                dma((LAYERS, PIECES)),
                 dma((3,)),
                 dma((3,)),
                 dma((2,)),
                 dma((2,)),
+                pltpu.SemaphoreType.REGULAR,
+                pltpu.SemaphoreType.REGULAR,
                 dma((LAYERS + 1, SETS)),
                 dma((SETS,)),
                 dma((LAYERS, SETS, CHIPS)),
@@ -472,6 +504,14 @@
             ),
         )(forcing, cotangent, flags, inverses)
     )
+    return tuple(
+        pl.pallas_call(
+            finish,
+            out_shape=[jax.ShapeDtypeStruct(forcing.shape, F32)] * 2,
+            in_specs=[vmem, vmem],
+            out_specs=[vmem, vmem],
+        )(*results)
+    )
 
 
 def solution(mesh):

time: 113 us -> 110 us (0.973); the launches traced: 112 us -> 110 us
  local copies, waits for them, and re-layouts: 2.95 us -> 0 us
    unnamed x2 -> x0, local copies, waits for them, and re-layouts: 2.95 us -> none
    pallas_call x0 -> x1, Pallas kernels: none -> 1.53 us  [shards(): pl.pallas_call(finish, out_shape=[jax.ShapeDtypeStruct(forcing.shape, F32...]
where the time goes in v4:
time: 110 us
  Pallas kernels  109 us (99%)
    pallas_call x1, Pallas kernels, shards(): pl.pallas_call(kernel, out_shape=[jax.ShapeDtypeStruct(forcing.shape, F32...  108 us

profile of v4, /device:TPU:1, one launch (start us, length us, event | category | flops | bytes accessed | tf_op | source)
XLA Modules:
  0.0 110.1 jit_solution(7398381700561871605)
XLA Ops:
  0.6 107.9 %shard_map.59 = (f32[4,32,128]{2,1,0:T(8,128)}, f32[4,32,128]{2,1,0:T(8,128)}) custom-call(f32[4,32,128]{2,1,0:T(8,128)} %forcing_in.1, f32[4,32,128]{2,1,0:T(8,128)} %cotangent_in.1, s32[4,64]{1,0:T(4,128)} %flags_in.1, f32[4,128,4096]{2,1,0:T(8,128)} %inverses.1), custom_call_target="tpu_custom_call" | custom-call | tf_op jit(solution)/shard_map/pallas_call | solution.py:453
  108.6 1.5 %shard_map.60 = (f32[4,32,128]{2,1,0:T(8,128)}, f32[4,32,128]{2,1,0:T(8,128)}) custom-call(f32[4,32,128]{2,1,0:T(8,128)} %get-tuple-element.4.response_in, f32[4,32,128]{2,1,0:T(8,128)} %get-tuple-element.5.gradient_in), custom_call_target="tpu_custom_call" | custom-call | tf_op jit(solution)/shard_map/pallas_call | solution.py:508
